TPU v7x, 32 devices: a whole 2x2x4 slice. The times are simulated.
32 devices in a mesh: res: 8 (over z, y), ch: 4 (over x, core).
Axes of the slice: x: 2, y: 2, z: 4, core: 2. Of those that a mesh axis runs over, the one named last changes fastest.
Arguments:
- sequence_matrix: bfloat16 [8, 512, 256], P(None, 'res'), may hold values from -6 to 6
- couple_matrix: bfloat16 [32, 128, 4096], P('res', 'ch')
- block_target_entry: int32 [8, 4], P('res'), may hold values from 0 to 7, as said below
- block_present_flag: int32 [8, 4], P('res'), may hold values from 0 to 1, as said below
- amino_strand: int32 [512], P('res'), may hold values from 0 to 5, never falling along the last dimension, each value on 1 to 170 neighbouring positions
- sequence_scaling_factor: float32 [256], replicated, may hold values from 0.5 to 1.5
- query_key_value_matrix: bfloat16 [4, 256, 256], P(None, None, 'ch'), may hold values from -0.375 to 0.375
- focus_result_matrix: bfloat16 [256, 256], P('ch'), may hold values from -0.375 to 0.375
- strand_focus_offset: float32 [8], replicated, may hold values from -2 to 2
- couple_scaling_factor: float32 [128], P('ch'), may hold values from 0.5 to 1.5
- focus_offset_matrix: float32 [128, 8], P('ch')
- product_scaling_factor: float32 [256], replicated, may hold values from 0.5 to 1.5
- first_factor_matrix: bfloat16 [256, 32], replicated, may hold values from -0.375 to 0.375
- second_factor_matrix: bfloat16 [256, 32], P(None, 'ch'), may hold values from -0.375 to 0.375
- product_result_matrix: bfloat16 [128, 32, 32], P(None, None, 'ch'), may hold values from -0.8984375 to 0.8984375
- product_result_offset: float32 [128], P('ch'), may hold values from -3 to 3
Outputs:
- sequence_result_matrix: bfloat16 [8, 512, 256], P(None, 'res')
- pairwise_output: bfloat16 [32, 128, 4096], P('res', 'ch')
Inputs may be any that keep to these rules, and one draw needn't show every extreme that they name: `block_target_entry`: slot 0 of row tile r names r itself; the column tiles of one row tile are distinct. `block_present_flag`: the valid slots of each row tile are its first ones, two or more of them; in every draw some row tile has all 4 slots valid.
All inputs are finite; a program needn't handle non-finite values.
Results may differ from a plain program's by a relative error of at most 0.005.
Values may be sent and summed in bfloat16 or wider, within the bound.
No kernel may reach another device: no remote copies, remote signals or barrier semaphores. Data moves between devices by JAX's collectives and lax.ppermute only.
A program may use at most 128 MiB of HBM per device.

v0:
```python
import math
import jax
import jax.numpy as jnp
from jax import lax
from jax.sharding import PartitionSpec as P

C_Z = 128
FOCUS_NUMBER = 8
FOCUS_BREADTH = 32
PRODUCT_FEATURE = 32
EPS = 1e-05
MASKED = -1e30


def final_dimension_standardize(values, gain_vector):
    values = values.astype(jnp.float32)
    average = jnp.mean(values, axis=-1, keepdims=True)
    variance = jnp.mean(jnp.square(values - average), axis=-1, keepdims=True)
    return (values - average) * lax.rsqrt(variance + EPS) * gain_vector


def on_device(
    sequence_matrix,
    couple_matrix,
    block_target_entry,
    block_present_flag,
    amino_strand,
    sequence_scaling_factor,
    query_key_value_matrix,
    focus_result_matrix,
    strand_focus_offset,
    couple_scaling_factor,
    focus_offset_matrix,
    product_scaling_factor,
    first_factor_matrix,
    second_factor_matrix,
    product_result_matrix,
    product_result_offset,
):
    groups = lax.axis_size("ch")
    group_index = lax.axis_index("ch")
    local_heads = FOCUS_NUMBER // groups
    slot_count = couple_matrix.shape[0]
    cell_count = couple_matrix.shape[2]
    block_extent = sequence_matrix.shape[1]
    sequence_number_overall = sequence_matrix.shape[0]
    pair_field = couple_matrix.astype(jnp.float32)
    part_one = jnp.sum(pair_field, axis=1)
    part_two = jnp.sum(pair_field * pair_field, axis=1)
    sum_one, sum_two = lax.psum((part_one, part_two), "ch")
    center = sum_one / C_Z
    spread = lax.rsqrt(sum_two / C_Z - center * center + EPS)
    normed = (
        (pair_field - center[:, None, :])
        * spread[:, None, :]
        * couple_scaling_factor[None, :, None]
    )
    partial_value = jnp.einsum(
        "kcp,ch->hkp", normed, focus_offset_matrix, precision=lax.Precision.HIGHEST
    )
    head_bias = lax.psum_scatter(partial_value, "ch", scatter_dimension=0, tiled=True)
    head_bias = head_bias.astype(jnp.bfloat16)
    bias_all, cols_all, valid_all, chain_all = (
        lax.all_gather(head_bias, "res", axis=1, tiled=True),
        lax.all_gather(block_target_entry, "res", axis=0, tiled=True),
        lax.all_gather(block_present_flag, "res", axis=0, tiled=True),
        lax.all_gather(amino_strand, "res", axis=0, tiled=True),
    )
    sequence_first_layout = lax.all_to_all(
        sequence_matrix, "res", split_axis=0, concat_axis=1, tiled=True
    )
    device_rows, amino_number_here, sequence_feature_breadth = sequence_first_layout.shape
    tile_count = amino_number_here // block_extent
    sequence_standardized = final_dimension_standardize(
        sequence_first_layout, sequence_scaling_factor
    ).astype(jnp.bfloat16)
    projected_rows = jnp.einsum(
        "hbx,sxt->shbt",
        sequence_standardized,
        query_key_value_matrix,
        preferred_element_type=jnp.float32,
    ).astype(jnp.bfloat16)
    projected_rows = projected_rows.reshape(
        4, device_rows, tile_count, block_extent, local_heads, FOCUS_BREADTH
    )
    queries = projected_rows[0]
    keyset = projected_rows[1]
    valueset = projected_rows[2]
    gateset = projected_rows[3]
    chain_tiles = chain_all.reshape(tile_count, block_extent)
    bias_tiles = bias_all.reshape(local_heads, tile_count, slot_count, block_extent, block_extent)
    head_scale = lax.dynamic_slice_in_dim(
        strand_focus_offset, group_index * local_heads, local_heads, 0
    )
    block_tiles = math.gcd(tile_count, max(1, 512 // block_extent))

    def attend(block_index):
        first_tile = block_index * block_tiles
        columns = lax.dynamic_slice_in_dim(cols_all, first_tile, block_tiles, 0)
        usable = lax.dynamic_slice_in_dim(valid_all, first_tile, block_tiles, 0) > 0
        query_block = lax.dynamic_slice_in_dim(queries, first_tile, block_tiles, 1)
        key_block = keyset[:, columns]
        value_block = valueset[:, columns]
        scores = jnp.einsum(
            "rgahd,rgkbhd->rghakb", query_block, key_block, preferred_element_type=jnp.float32
        ) * FOCUS_BREADTH ** (-0.5)
        pair_part = lax.dynamic_slice_in_dim(bias_tiles, first_tile, block_tiles, 1).astype(
            jnp.float32
        )
        pair_part = pair_part.transpose(1, 0, 3, 2, 4)
        query_chain = lax.dynamic_slice_in_dim(chain_tiles, first_tile, block_tiles, 0)
        same_chain = (query_chain[:, :, None, None] == chain_tiles[columns][:, None, :, :]).astype(
            jnp.float32
        )
        scores = (
            scores
            + pair_part[None]
            + head_scale[None, None, :, None, None, None] * same_chain[None, :, None]
        )
        scores = jnp.where(usable[None, :, None, None, :, None], scores, MASKED)
        row_max = jnp.max(scores, axis=(4, 5), keepdims=True)
        exponent = jnp.exp(scores - row_max)
        attn_weights = (exponent / jnp.sum(exponent, axis=(4, 5), keepdims=True)).astype(
            jnp.bfloat16
        )
        mixed = jnp.einsum(
            "rghakb,rgkbhd->rgahd", attn_weights, value_block, preferred_element_type=jnp.float32
        )
        gate_block = lax.dynamic_slice_in_dim(gateset, first_tile, block_tiles, 1).astype(
            jnp.float32
        )
        return (mixed * jax.nn.sigmoid(gate_block)).astype(jnp.bfloat16)

    blocks = lax.map(attend, jnp.arange(tile_count // block_tiles, dtype=jnp.int32))
    attended_rows = blocks.transpose(1, 0, 2, 3, 4, 5).reshape(
        device_rows * amino_number_here, local_heads * FOCUS_BREADTH
    )
    residual_input = sequence_first_layout.reshape(
        device_rows * amino_number_here, sequence_feature_breadth
    )
    partial_out = jnp.dot(attended_rows, focus_result_matrix, preferred_element_type=jnp.float32)
    head_total = lax.psum(partial_out, "ch")
    updated_state = (
        (residual_input.astype(jnp.float32) + head_total)
        .astype(jnp.bfloat16)
        .reshape(device_rows, amino_number_here, sequence_feature_breadth)
    )
    sequence_result_matrix = lax.all_to_all(
        updated_state, "res", split_axis=1, concat_axis=0, tiled=True
    )
    outer_normed = (
        final_dimension_standardize(sequence_result_matrix, product_scaling_factor)
        .astype(jnp.bfloat16)
        .reshape(sequence_number_overall * block_extent, sequence_feature_breadth)
    )
    left_projected = (
        jnp.dot(outer_normed, first_factor_matrix, preferred_element_type=jnp.float32)
        .astype(jnp.bfloat16)
        .reshape(sequence_number_overall, block_extent * PRODUCT_FEATURE)
    )
    own_columns = block_target_entry[0]
    right_projected = (
        jnp.dot(outer_normed, second_factor_matrix, preferred_element_type=jnp.float32)
        .astype(jnp.bfloat16)
        .reshape(sequence_number_overall, block_extent, -1)
    )
    narrow = right_projected.shape[2]
    weight_flat = product_result_matrix.reshape(C_Z, PRODUCT_FEATURE * narrow)
    empty_tiles = jnp.zeros(
        (slot_count, sequence_number_overall, block_extent, narrow), jnp.bfloat16
    )
    shard_piece = lax.all_gather(right_projected, "res", axis=1, tiled=True)
    piece_rows = shard_piece.shape[1]
    offset = own_columns * block_extent
    inside = (offset >= 0) & (offset < piece_rows)

    def take_one(offset_one, inside_one, held_tile):
        taken = lax.dynamic_slice_in_dim(
            shard_piece, jnp.clip(offset_one, 0, piece_rows - block_extent), block_extent, 1
        )
        return jnp.where(inside_one, taken, held_tile)

    chosen = jax.vmap(take_one, in_axes=(0, 0, 0))(offset, inside, empty_tiles)
    left_turned = left_projected.T

    def outer_one(right_tile_rows):
        product = (
            jnp.dot(
                left_turned,
                right_tile_rows.reshape(sequence_number_overall, block_extent * narrow),
                preferred_element_type=jnp.float32,
            )
            / sequence_number_overall
        )
        product = (
            product.reshape(block_extent, PRODUCT_FEATURE, block_extent, narrow)
            .transpose(1, 3, 0, 2)
            .astype(jnp.bfloat16)
            .reshape(PRODUCT_FEATURE * narrow, cell_count)
        )
        return jnp.dot(weight_flat, product, preferred_element_type=jnp.float32)

    partials = lax.map(outer_one, chosen)
    summed = lax.psum_scatter(partials, "ch", scatter_dimension=1, tiled=True)
    keep_mask = block_present_flag[0].astype(jnp.float32)
    pairwise_output = (
        pair_field + keep_mask[:, None, None] * (summed + product_result_offset[None, :, None])
    ).astype(jnp.bfloat16)
    return (sequence_result_matrix, pairwise_output)


def solution(mesh):
    return jax.shard_map(
        on_device,
        mesh=mesh,
        in_specs=(
            P(None, "res", None),
            P("res", "ch", None),
            P("res", None),
            P("res", None),
            P("res"),
            P(),
            P(None, None, "ch"),
            P("ch", None),
            P(),
            P("ch"),
            P("ch", None),
            P(),
            P(),
            P(None, "ch"),
            P(None, None, "ch"),
            P("ch"),
        ),
        out_specs=(P(None, "res", None), P("res", "ch", None)),
        check_vma=False,
    )
```

profile of v0, /device:TPU:0, one launch (start us, length us, event | category | flops | bytes accessed | tf_op | source)
XLA Modules:
  0.0 450.4 jit_solution(9530738559762649015)
XLA Ops:
  7.2 7.5 %all-to-all-start = ((bf16[8,64,256]{2,1,0:T(8,128)(2,1)}), bf16[8,64,256]{2,1,0:T(8,128)(2,1)S(1)}, u32[]{:S(2)}, u32[]{:S(2)}) async-start(bf16[8,64,256]{2,1,0:T(8,128)(2,1)} %param.18), calls=%async_computation | async-start | bytes 524288 | tf_op jit(solution)/shard_map/all_to_all | solution.py:69
  14.7 2.4 convert_reduce_fusion
  17.2 1.2 dynamic-slice
  19.1 0.9 dynamic-update-slice
  20.0 11.8 %all-reduce = s32[512]{0:T(512)S(1)} all-reduce(s32[512]{0:T(512)S(1)} %dynamic-update-slice), channel_id=1, replica_groups=mesh['res'=8,'ch'=4] {'res'}, use_global_device_ids=true, to_apply=%add | all-reduce | flops 512 | bytes 4096
  31.9 17.9 %all-gather = s32[8,1,4]{2,1,0:T(1,128)S(1)} all-gather(s32[1,1,4]{2,1,0:T(1,128)} %bitcast.164), channel_id=1, replica_groups=mesh['res'=8,'ch'=4] {'res'}, dimensions={0}, use_global_device_ids=true | all-gather | bytes 144 | tf_op jit(solution)/shard_map/all_gather | solution.py:65
  50.6 1.3 compare_convert_fusion
  51.9 16.8 %all-gather.1 = s32[8,1,4]{2,1,0:T(1,128)S(1)} all-gather(s32[1,1,4]{2,1,0:T(1,128)S(1)} %bitcast.165), channel_id=1, replica_groups=mesh['res'=8,'ch'=4] {'res'}, dimensions={0}, use_global_device_ids=true | all-gather | bytes 144 | tf_op jit(solution)/shard_map/all_gather | solution.py:66
  69.0 0.6 dynamic-slice.1
  70.3 0.9 broadcast_multiply_fusion
  71.2 1.5 convolution_bitcast_fusion.1
  73.0 16.4 %all-reduce.10 = bf16[8,4,4096]{2,1,0:T(4,128)(2,1)S(1)} all-reduce(f32[8,4,4096]{2,1,0:T(4,128)S(1)} %copy.104), channel_id=2, replica_groups=mesh['res'=8,'ch'=4] {'ch'}, use_global_device_ids=true, to_apply=%region_6.0.clone | all-reduce | flops 131072 | bytes 786432
  89.5 31.4 %all_gather.17 = bf16[2,32,4096]{2,0,1:T(2,128)(2,1)S(1)} all-gather(bf16[2,4,4096]{2,0,1:T(2,128)(2,1)S(1)} %copy.105), channel_id=1, replica_groups=mesh['res'=8,'ch'=4] {'res'}, dimensions={1}, use_global_device_ids=true | all-gather | bytes 589824 | tf_op jit(solution)/shard_map/all_gather | solution.py:64
  121.3 2.2 reshape.314
  123.5 1.9 copy.107
  127.3 0.6 gather_fusion.1
  128.1 1.0 reshape.315
  129.1 1.4 gather_fusion
  130.5 0.8 reshape.312
  131.3 2.1 fusion.31
  133.8 0.7 copy-done.3
  135.3 1.0 fusion.33
  136.4 31.8 %all-reduce.7.cloned.1.call-done = f32[512,256]{1,0:T(8,128)} async-done(((f32[512,256]{1,0:T(8,128)}), f32[512,256]{1,0:T(8,128)}) %all-reduce.7.cloned.1.call-update) | async-done | bytes 524304 | tf_op jit(solution)/shard_map/psum | solution.py:142
  168.2 1.1 fusion.22
  170.2 2.2 reduce.8
  172.4 0.8 reshape.378
  173.2 5.6 %all-to-all-start.1 = ((bf16[8,2,8192]{2,1,0:T(2,128)(2,1)}), bf16[8,2,8192]{2,1,0:T(2,128)(2,1)S(1)}, u32[]{:S(2)}, u32[]{:S(2)}) async-start(bf16[8,2,8192]{2,1,0:T(2,128)(2,1)} %reshape.378), calls=%async_computation.1 | async-start | bytes 524288 | tf_op jit(solution)/shard_map/all_to_all | solution.py:148
  179.1 8.0 %all-to-all-done.1 = bf16[8,2,8192]{2,1,0:T(2,128)(2,1)S(1)} async-done(((bf16[8,2,8192]{2,1,0:T(2,128)(2,1)}), bf16[8,2,8192]{2,1,0:T(2,128)(2,1)S(1)}, u32[]{:S(2)}, u32[]{:S(2)}) %all-to-all-start.1) | async-done | bytes 262176 | tf_op jit(solution)/shard_map/all_to_all | solution.py:148
  187.9 1.3 convert_reduce_fusion.2
  189.2 7.4 %multiply_reduce_fusion = f32[512]{0:T(512)S(1)} fusion(f32[512]{0:T(512)S(1)} %broadcast_multiply_fusion.2, bf16[512,1,256]{2,1,0:T(2,128)(2,1)S(1)} %reshape.379), kind=kLoop, calls=%fused_computation.49 | loop fusion | flops 523776 | bytes 266240 | tf_op jit(solution)/shard_map/reduce_sum | solution.py:18
  197.2 33.1 %all_gather.19 = bf16[8,512,8]{2,0,1:T(8,128)(2,1)S(1)} all-gather(bf16[8,64,8]{2,0,1:T(8,128)(2,1)S(1)} %copy.113), channel_id=1, replica_groups=mesh['res'=8,'ch'=4] {'res'}, dimensions={1}, use_global_device_ids=true | all-gather | bytes 73728 | tf_op jit(solution)/shard_map/all_gather | solution.py:172
  230.8 0.7 gather_fusion.3
  231.6 139.8 %while.2 = (s32[]{:T(128)}, f32[4,128,4096]{2,1,0:T(8,128)}, bf16[4,8,64,8]{3,1,2,0:T(8,128)(2,1)S(1)}, bf16[2048,8]{0,1:T(8,128)(2,1)S(1)}, bf16[128,256]{1,0:T(8,128)(2,1)S(1)}, /*index=5*/s32[]{:T(128)}) while((s32[]{:T(128)}, f32[4,128,4096]{2,1,0:T(8,128)}, bf16[4,8,64,8]{3,1,2,0:T(8,128)(2,1)S(1)}, bf16[2048,8]{0,1:T(8,128)(2,1)S(1)}, ...), condition=%wide.region_13.14_spmd, body=%wide.region_12.13_spmd.sunk | while | flops 287309824 | bytes 27418708 | solution.py:203
  231.8 0.8 fusion.55
  232.6 8.1 %convert_element_type.203 = bf16[64,32,64,8]{1,0,3,2:T(8,128)(2,1)} reshape(bf16[2048,512]{0,1:T(8,128)(2,1)S(1)} %fusion.55) | data formatting | bytes 4194304 | tf_op jit(solution)/shard_map/while/body/eval_jaxpr/convert_element_type | solution.py:198
  240.7 14.6 %copy.154 = bf16[32,8,64,64]{3,2,1,0:T(8,128)(2,1)} copy(bf16[32,8,64,64]{0,2,1,3:T(8,128)(2,1)} %bitcast.151) | data formatting | bytes 4194304 | tf_op jit(solution)/shard_map/while/body/eval_jaxpr/convert_element_type | solution.py:198
  255.3 5.7 %reshape.383 = bf16[256,4096]{1,0:T(8,128)(2,1)S(1)} reshape(bf16[32,8,64,64]{3,2,1,0:T(8,128)(2,1)} %copy.154) | data formatting | bytes 4194304 | tf_op jit(solution)/shard_map/while/body/eval_jaxpr/reshape | solution.py:199
  261.0 2.2 convolution_bitcast_fusion.4
  263.1 1.9 copy.155
  265.1 1.5 constant_dynamic-update-slice_fusion.2
  266.8 0.8 fusion.55
  267.6 8.1 %convert_element_type.203 = bf16[64,32,64,8]{1,0,3,2:T(8,128)(2,1)} reshape(bf16[2048,512]{0,1:T(8,128)(2,1)S(1)} %fusion.55) | data formatting | bytes 4194304 | tf_op jit(solution)/shard_map/while/body/eval_jaxpr/convert_element_type | solution.py:198
  275.7 14.6 %copy.154 = bf16[32,8,64,64]{3,2,1,0:T(8,128)(2,1)} copy(bf16[32,8,64,64]{0,2,1,3:T(8,128)(2,1)} %bitcast.151) | data formatting | bytes 4194304 | tf_op jit(solution)/shard_map/while/body/eval_jaxpr/convert_element_type | solution.py:198
  290.3 5.7 %reshape.383 = bf16[256,4096]{1,0:T(8,128)(2,1)S(1)} reshape(bf16[32,8,64,64]{3,2,1,0:T(8,128)(2,1)} %copy.154) | data formatting | bytes 4194304 | tf_op jit(solution)/shard_map/while/body/eval_jaxpr/reshape | solution.py:199
  296.0 2.2 convolution_bitcast_fusion.4
  298.1 1.9 copy.155
  300.1 1.4 constant_dynamic-update-slice_fusion.2
  301.7 0.8 fusion.55
  302.5 8.1 %convert_element_type.203 = bf16[64,32,64,8]{1,0,3,2:T(8,128)(2,1)} reshape(bf16[2048,512]{0,1:T(8,128)(2,1)S(1)} %fusion.55) | data formatting | bytes 4194304 | tf_op jit(solution)/shard_map/while/body/eval_jaxpr/convert_element_type | solution.py:198
  310.6 14.6 %copy.154 = bf16[32,8,64,64]{3,2,1,0:T(8,128)(2,1)} copy(bf16[32,8,64,64]{0,2,1,3:T(8,128)(2,1)} %bitcast.151) | data formatting | bytes 4194304 | tf_op jit(solution)/shard_map/while/body/eval_jaxpr/convert_element_type | solution.py:198
  325.2 5.7 %reshape.383 = bf16[256,4096]{1,0:T(8,128)(2,1)S(1)} reshape(bf16[32,8,64,64]{3,2,1,0:T(8,128)(2,1)} %copy.154) | data formatting | bytes 4194304 | tf_op jit(solution)/shard_map/while/body/eval_jaxpr/reshape | solution.py:199
  330.9 2.2 convolution_bitcast_fusion.4
  333.0 1.9 copy.155
  335.0 1.5 constant_dynamic-update-slice_fusion.2
  336.7 0.8 fusion.55
  337.4 8.1 %convert_element_type.203 = bf16[64,32,64,8]{1,0,3,2:T(8,128)(2,1)} reshape(bf16[2048,512]{0,1:T(8,128)(2,1)S(1)} %fusion.55) | data formatting | bytes 4194304 | tf_op jit(solution)/shard_map/while/body/eval_jaxpr/convert_element_type | solution.py:198
  345.6 14.6 %copy.154 = bf16[32,8,64,64]{3,2,1,0:T(8,128)(2,1)} copy(bf16[32,8,64,64]{0,2,1,3:T(8,128)(2,1)} %bitcast.151) | data formatting | bytes 4194304 | tf_op jit(solution)/shard_map/while/body/eval_jaxpr/convert_element_type | solution.py:198
  360.2 5.7 %reshape.383 = bf16[256,4096]{1,0:T(8,128)(2,1)S(1)} reshape(bf16[32,8,64,64]{3,2,1,0:T(8,128)(2,1)} %copy.154) | data formatting | bytes 4194304 | tf_op jit(solution)/shard_map/while/body/eval_jaxpr/reshape | solution.py:199
  365.8 2.2 convolution_bitcast_fusion.4
  368.0 1.9 copy.155
  369.9 1.5 constant_dynamic-update-slice_fusion.2
  371.5 0.7 copy.126
  372.2 68.8 %reduce-scatter.2.cloned.1.call-done = f32[4,32,4096]{2,1,0:T(8,128)} async-done(((f32[4,128,4096]{2,1,0:T(8,128)}), f32[4,32,4096]{2,1,0:T(8,128)}) %reduce-scatter.2.cloned.1.call-update) | async-done | bytes 2097168 | tf_op jit(solution)/shard_map/reduce_scatter | solution.py:204
  441.0 3.0 fusion.5
  (109 shorter events, 9.3 us)
Async XLA Ops:
  7.2 119.0 %copy-start = (bf16[4,256,64]{1,2,0:T(8,128)(2,1)S(1)}, bf16[4,256,64]{1,2,0:T(8,128)(2,1)}, u32[]{:S(2)}) copy-start(bf16[4,256,64]{1,2,0:T(8,128)(2,1)} %param.24) | copy-start | bytes 393220
  7.2 61.8 %copy-start.17 = (u32[32]{0:T(128)S(1)}, u32[32]{0:T(128)}, u32[]{:S(2)}) copy-start(u32[32]{0:T(128)} %constant.112) | copy-start | bytes 388
  7.2 64.0 %copy-start.1 = (bf16[4,32,4096]{2,1,0:T(8,128)(2,1)S(1)}, bf16[4,32,4096]{2,1,0:T(8,128)(2,1)}, u32[]{:S(2)}) copy-start(bf16[4,32,4096]{2,1,0:T(8,128)(2,1)} %param.19) | copy-start | bytes 3145732
  7.2 44.7 %copy-start.13 = (s32[1,4]{1,0:T(1,128)S(1)}, s32[1,4]{1,0:T(1,128)}, u32[]{:S(2)}) copy-start(s32[1,4]{1,0:T(1,128)} %param.21) | copy-start | bytes 52
  7.2 61.7 %copy-start.15 = (f32[8]{0:T(128)S(1)}, f32[8]{0:T(128)}, u32[]{:S(2)}) copy-start(f32[8]{0:T(128)} %param.26) | copy-start | bytes 100
  7.2 64.0 %copy-start.16 = (f32[32]{0:T(128)S(1)}, f32[32]{0:T(128)}, u32[]{:S(2)}) copy-start(f32[32]{0:T(128)} %param.27) | copy-start | bytes 388
  7.2 64.0 %copy-start.14 = (f32[32,8]{0,1:T(8,128)S(1)}, f32[32,8]{0,1:T(8,128)}, u32[]{:S(2)}) copy-start(f32[32,8]{0,1:T(8,128)} %param.28) | copy-start | bytes 3076
  7.2 118.2 %all-to-all-start = ((bf16[8,64,256]{2,1,0:T(8,128)(2,1)}), bf16[8,64,256]{2,1,0:T(8,128)(2,1)S(1)}, u32[]{:S(2)}, u32[]{:S(2)}) async-start(bf16[8,64,256]{2,1,0:T(8,128)(2,1)} %param.18), calls=%async_computation | async-start | bytes 524288 | tf_op jit(solution)/shard_map/all_to_all | solution.py:69
  14.7 55.5 %all-reduce.9.cloned.1.call-start = ((), (), s32[]{:S(2)}) async-start(), calls=%async_computation.5 | async-start | bytes 262144 | tf_op jit(solution)/shard_map/psum | solution.py:50
  17.1 151.0 %all-reduce.7.cloned.1.call-start = ((), (), s32[]{:S(2)}) async-start(), calls=%async_computation.3 | async-start | bytes 1048576 | tf_op jit(solution)/shard_map/psum | solution.py:142
  123.5 2.5 copy-start.9
  133.4 1.0 copy-start.3
  133.4 1.1 copy-start.4
  134.5 0.8 copy-start.6
  136.3 42.6 %copy-start.5 = (bf16[128,32,8]{0,2,1:T(8,128)(2,1)S(1)}, bf16[128,32,8]{0,2,1:T(8,128)(2,1)}, u32[]{:S(2)}) copy-start(bf16[128,32,8]{0,2,1:T(8,128)(2,1)} %param.32) | copy-start | bytes 196612
  136.3 42.7 %copy-start.12 = (s32[1,4]{1,0:T(1,128)S(1)}, s32[1,4]{1,0:T(1,128)}, u32[]{:S(2)}) copy-start(s32[1,4]{1,0:T(1,128)} %param.20) | copy-start | bytes 52
  172.4 24.2 %copy-start.10 = (f32[256]{0:T(256)S(1)}, f32[256]{0:T(256)}, u32[]{:S(2)}) copy-start(f32[256]{0:T(256)} %param.29) | copy-start | bytes 3076
  173.2 23.6 %copy-start.8 = (bf16[256,8]{0,1:T(8,128)(2,1)S(1)}, bf16[256,8]{0,1:T(8,128)(2,1)}, u32[]{:S(2)}) copy-start(bf16[256,8]{0,1:T(8,128)(2,1)} %param.31) | copy-start | bytes 12292
  173.2 13.9 %all-to-all-start.1 = ((bf16[8,2,8192]{2,1,0:T(2,128)(2,1)}), bf16[8,2,8192]{2,1,0:T(2,128)(2,1)S(1)}, u32[]{:S(2)}, u32[]{:S(2)}) async-start(bf16[8,2,8192]{2,1,0:T(2,128)(2,1)} %reshape.378), calls=%async_computation.1 | async-start | bytes 524288 | tf_op jit(solution)/shard_map/all_to_all | solution.py:148
  178.8 262.1 %reduce-scatter.2.cloned.1.call-start = ((), (), s32[]{:S(2)}) async-start(), calls=%async_computation.4 | async-start | bytes 10485760 | tf_op jit(solution)/shard_map/reduce_scatter | solution.py:204
  187.3 43.0 %copy-start.7 = (bf16[256,32]{0,1:T(8,128)(2,1)S(1)}, bf16[256,32]{0,1:T(8,128)(2,1)}, u32[]{:S(2)}) copy-start(bf16[256,32]{0,1:T(8,128)(2,1)} %param.30) | copy-start | bytes 49156
  371.4 69.5 %copy-start.2 = (bf16[4,32,4096]{2,1,0:T(8,128)(2,1)S(1)}, bf16[4,32,4096]{2,1,0:T(8,128)(2,1)}, u32[]{:S(2)}) copy-start(bf16[4,32,4096]{2,1,0:T(8,128)(2,1)} %param.19) | copy-start | bytes 3145732
  371.4 69.5 %copy-start.11 = (f32[32]{0:T(128)S(1)}, f32[32]{0:T(128)}, u32[]{:S(2)}) copy-start(f32[32]{0:T(128)} %param.33) | copy-start | bytes 388
Sparse Core Ops, SparseCore 0:
  18.5 33.1 all-reduce.8
  136.5 31.6 all-reduce.6
  371.6 69.3 reduce-scatter.1
where the time goes:
time: 452 us; the launch traced here: 450 us
  local copies, waits for them, and re-layouts  146 us (32%)
  blocking collectives  127 us (28%)
  waiting for transfers between devices  109 us (24%)
  other arithmetic  21.8 us (5%)
  matrix products  17.3 us (4%)
  between operations  15.5 us (3%)
  starting transfers between devices  13.2 us (3%)
    convert_element_type x8, local copies, waits for them, and re-layouts, outer_one(): product = product.reshape(block_extent, PRODUCT_FEATURE, block_extent, na...  90.9 us
    reduce_scatter x1, waiting for transfers between devices, on_device(): summed = lax.psum_scatter(partials, 'ch', scatter_dimension=1, tiled=True)  68.8 us
    all_gather x1, blocking collectives, on_device(): shard_piece = lax.all_gather(right_projected, 'res', axis=1, tiled=True)  33.1 us
    psum x1, waiting for transfers between devices, on_device(): head_total = lax.psum(partial_out, 'ch')  31.8 us
    all_gather x1, blocking collectives, on_device(): lax.all_gather(head_bias, 'res', axis=1, tiled=True)  31.4 us
    unnamed x2, blocking collectives  28.2 us
    reshape x4, local copies, waits for them, and re-layouts, outer_one(): product = product.reshape(block_extent, PRODUCT_FEATURE, block_extent, na...  22.7 us
    all_gather x1, blocking collectives, on_device(): lax.all_gather(block_target_entry, 'res', axis=0, tiled=True)  17.9 us
  transfers between devices with their start and end apart: 5, of which 3 were waited for; matrix products, arithmetic and copies ran while one was open for 4% of the time, Pallas kernels for 0%

commit v1 on v0

--- a/solution.py
+++ b/solution.py
@@ -139,7 +139,11 @@
         device_rows * amino_number_here, sequence_feature_breadth
     )
     partial_out = jnp.dot(attended_rows, focus_result_matrix, preferred_element_type=jnp.float32)
-    head_total = lax.psum(partial_out, "ch")
+    head_total = partial_out
+    for hop in (1, 2):
+        head_total = head_total + lax.ppermute(
+            head_total, "ch", [(dev, dev ^ hop) for dev in range(4)]
+        )
     updated_state = (
         (residual_input.astype(jnp.float32) + head_total)
         .astype(jnp.bfloat16)

time: 452 us -> 434 us (0.960)
  waiting for transfers between devices: 109 us -> 91.8 us
    psum x1 -> x0, waiting for transfers between devices: 31.8 us -> none  [on_device(): head_total = lax.psum(partial_out, 'ch')]
    ppermute x0 -> x2, waiting for transfers between devices: none -> 14.2 us  [on_device(): lax.ppermute(head_total, 'ch', [(dev, dev ^ hop) for dev in range(4)])]
  transfers between devices with their start and end apart: 5 -> 6, of which waited for: 3 -> 4; matrix products, arithmetic and copies ran while one was open for 4% -> 4% of each run, Pallas kernels for 0% -> 0%
where the time goes in v1:
time: 434 us; the launch traced here: 432 us
  local copies, waits for them, and re-layouts  146 us (34%)
  blocking collectives  128 us (29%)
  waiting for transfers between devices  91.8 us (21%)
  other arithmetic  20.9 us (5%)
  matrix products  16.5 us (4%)
  between operations  15.8 us (4%)
  starting transfers between devices  13.1 us (3%)
    convert_element_type x8, local copies, waits for them, and re-layouts, outer_one(): product = product.reshape(block_extent, PRODUCT_FEATURE, block_extent, na...  90.9 us
    reduce_scatter x1, waiting for transfers between devices, on_device(): summed = lax.psum_scatter(partials, 'ch', scatter_dimension=1, tiled=True)  69.3 us
    all_gather x1, blocking collectives, on_device(): shard_piece = lax.all_gather(right_projected, 'res', axis=1, tiled=True)  33.2 us
    all_gather x1, blocking collectives, on_device(): lax.all_gather(head_bias, 'res', axis=1, tiled=True)  31.6 us
    unnamed x2, blocking collectives  28.2 us
    reshape x4, local copies, waits for them, and re-layouts, outer_one(): product = product.reshape(block_extent, PRODUCT_FEATURE, block_extent, na...  22.7 us
    all_gather x1, blocking collectives, on_device(): lax.all_gather(block_target_entry, 'res', axis=0, tiled=True)  17.9 us
    all_gather x1, blocking collectives, on_device(): lax.all_gather(block_present_flag, 'res', axis=0, tiled=True)  16.8 us
  transfers between devices with their start and end apart: 6, of which 4 were waited for; matrix products, arithmetic and copies ran while one was open for 4% of the time, Pallas kernels for 0%

profile of v1, /device:TPU:0, one launch (start us, length us, event | category | flops | bytes accessed | tf_op | source)
XLA Modules:
  0.0 432.3 jit_solution(13230358237185332678)
XLA Ops:
  7.2 7.5 %all-to-all-start = ((bf16[8,64,256]{2,1,0:T(8,128)(2,1)}), bf16[8,64,256]{2,1,0:T(8,128)(2,1)S(1)}, u32[]{:S(2)}, u32[]{:S(2)}) async-start(bf16[8,64,256]{2,1,0:T(8,128)(2,1)} %param.18), calls=%async_computation | async-start | bytes 524288 | tf_op jit(solution)/shard_map/all_to_all | solution.py:69
  14.7 2.4 convert_reduce_fusion
  17.1 1.2 dynamic-slice
  19.1 0.9 dynamic-update-slice
  19.9 11.8 %all-reduce = s32[512]{0:T(512)S(1)} all-reduce(s32[512]{0:T(512)S(1)} %dynamic-update-slice), channel_id=1, replica_groups=mesh['res'=8,'ch'=4] {'res'}, use_global_device_ids=true, to_apply=%add | all-reduce | flops 512 | bytes 4096
  31.8 17.9 %all-gather = s32[8,1,4]{2,1,0:T(1,128)S(1)} all-gather(s32[1,1,4]{2,1,0:T(1,128)} %bitcast.164), channel_id=1, replica_groups=mesh['res'=8,'ch'=4] {'res'}, dimensions={0}, use_global_device_ids=true | all-gather | bytes 144 | tf_op jit(solution)/shard_map/all_gather | solution.py:65
  50.5 1.3 compare_convert_fusion
  51.9 16.8 %all-gather.1 = s32[8,1,4]{2,1,0:T(1,128)S(1)} all-gather(s32[1,1,4]{2,1,0:T(1,128)S(1)} %bitcast.165), channel_id=1, replica_groups=mesh['res'=8,'ch'=4] {'res'}, dimensions={0}, use_global_device_ids=true | all-gather | bytes 144 | tf_op jit(solution)/shard_map/all_gather | solution.py:66
  68.9 0.6 dynamic-slice.1
  70.2 0.9 broadcast_multiply_fusion
  71.1 1.5 convolution_bitcast_fusion.1
  73.0 16.4 %all-reduce.7 = bf16[8,4,4096]{2,1,0:T(4,128)(2,1)S(1)} all-reduce(f32[8,4,4096]{2,1,0:T(4,128)S(1)} %copy.104), channel_id=2, replica_groups=mesh['res'=8,'ch'=4] {'ch'}, use_global_device_ids=true, to_apply=%region_6.0.clone | all-reduce | flops 131072 | bytes 786432
  89.5 31.6 %all_gather.17 = bf16[2,32,4096]{2,0,1:T(2,128)(2,1)S(1)} all-gather(bf16[2,4,4096]{2,0,1:T(2,128)(2,1)S(1)} %copy.105), channel_id=1, replica_groups=mesh['res'=8,'ch'=4] {'res'}, dimensions={1}, use_global_device_ids=true | all-gather | bytes 589824 | tf_op jit(solution)/shard_map/all_gather | solution.py:64
  121.4 2.2 reshape.314
  123.6 1.9 copy.107
  127.5 0.6 gather_fusion.1
  128.2 1.0 reshape.315
  129.3 1.4 gather_fusion
  130.7 0.8 reshape.312
  131.5 2.1 fusion.31
  133.9 0.7 copy-done.3
  135.8 1.9 collective-permute-done
  137.7 1.7 collective-permute-start.1
  139.4 12.3 %collective-permute-done.1 = f32[512,256]{1,0:T(8,128)S(1)} collective-permute-done((f32[512,256]{1,0:T(8,128)S(1)}, f32[512,256]{1,0:T(8,128)S(1)}, u32[]{:S(2)}, u32[]{:S(2)}) %collective-permute-start.1) | collective-permute-done | bytes 524320 | tf_op jit(solution)/shard_map/ppermute | solution.py:144
  152.8 2.2 reduce.8
  155.0 0.8 reshape.378
  155.8 3.5 all-to-all-start.1
  159.8 8.1 %all-to-all-done.1 = bf16[8,2,8192]{2,1,0:T(2,128)(2,1)S(1)} async-done(((bf16[8,2,8192]{2,1,0:T(2,128)(2,1)}), bf16[8,2,8192]{2,1,0:T(2,128)(2,1)S(1)}, u32[]{:S(2)}, u32[]{:S(2)}) %all-to-all-start.1) | async-done | bytes 262176 | tf_op jit(solution)/shard_map/all_to_all | solution.py:152
  168.8 1.3 convert_reduce_fusion.2
  170.0 7.4 %multiply_reduce_fusion = f32[512]{0:T(512)S(1)} fusion(f32[512]{0:T(512)S(1)} %broadcast_multiply_fusion.2, bf16[512,1,256]{2,1,0:T(2,128)(2,1)S(1)} %reshape.379), kind=kLoop, calls=%fused_computation.49 | loop fusion | flops 523776 | bytes 266240 | tf_op jit(solution)/shard_map/reduce_sum | solution.py:18
  178.1 33.2 %all_gather.19 = bf16[8,512,8]{2,0,1:T(8,128)(2,1)S(1)} all-gather(bf16[8,64,8]{2,0,1:T(8,128)(2,1)S(1)} %copy.113), channel_id=1, replica_groups=mesh['res'=8,'ch'=4] {'res'}, dimensions={1}, use_global_device_ids=true | all-gather | bytes 73728 | tf_op jit(solution)/shard_map/all_gather | solution.py:176
  211.8 0.7 gather_fusion.3
  212.5 139.8 %while.2 = (s32[]{:T(128)}, f32[4,128,4096]{2,1,0:T(8,128)}, bf16[4,8,64,8]{3,1,2,0:T(8,128)(2,1)S(1)}, bf16[2048,8]{0,1:T(8,128)(2,1)S(1)}, bf16[128,256]{1,0:T(8,128)(2,1)S(1)}, /*index=5*/s32[]{:T(128)}) while((s32[]{:T(128)}, f32[4,128,4096]{2,1,0:T(8,128)}, bf16[4,8,64,8]{3,1,2,0:T(8,128)(2,1)S(1)}, bf16[2048,8]{0,1:T(8,128)(2,1)S(1)}, ...), condition=%wide.region_12.13_spmd, body=%wide.region_11.12_spmd.sunk | while | flops 287309824 | bytes 27418708 | solution.py:207
  212.8 0.8 fusion.55
  213.6 8.1 %convert_element_type.203 = bf16[64,32,64,8]{1,0,3,2:T(8,128)(2,1)} reshape(bf16[2048,512]{0,1:T(8,128)(2,1)S(1)} %fusion.55) | data formatting | bytes 4194304 | tf_op jit(solution)/shard_map/while/body/eval_jaxpr/convert_element_type | solution.py:202
  221.7 14.6 %copy.154 = bf16[32,8,64,64]{3,2,1,0:T(8,128)(2,1)} copy(bf16[32,8,64,64]{0,2,1,3:T(8,128)(2,1)} %bitcast.151) | data formatting | bytes 4194304 | tf_op jit(solution)/shard_map/while/body/eval_jaxpr/convert_element_type | solution.py:202
  236.3 5.7 %reshape.383 = bf16[256,4096]{1,0:T(8,128)(2,1)S(1)} reshape(bf16[32,8,64,64]{3,2,1,0:T(8,128)(2,1)} %copy.154) | data formatting | bytes 4194304 | tf_op jit(solution)/shard_map/while/body/eval_jaxpr/reshape | solution.py:203
  242.0 2.2 convolution_bitcast_fusion.4
  244.1 1.9 copy.155
  246.0 1.5 constant_dynamic-update-slice_fusion.2
  247.8 0.8 fusion.55
  248.5 8.1 %convert_element_type.203 = bf16[64,32,64,8]{1,0,3,2:T(8,128)(2,1)} reshape(bf16[2048,512]{0,1:T(8,128)(2,1)S(1)} %fusion.55) | data formatting | bytes 4194304 | tf_op jit(solution)/shard_map/while/body/eval_jaxpr/convert_element_type | solution.py:202
  256.7 14.6 %copy.154 = bf16[32,8,64,64]{3,2,1,0:T(8,128)(2,1)} copy(bf16[32,8,64,64]{0,2,1,3:T(8,128)(2,1)} %bitcast.151) | data formatting | bytes 4194304 | tf_op jit(solution)/shard_map/while/body/eval_jaxpr/convert_element_type | solution.py:202
  271.3 5.7 %reshape.383 = bf16[256,4096]{1,0:T(8,128)(2,1)S(1)} reshape(bf16[32,8,64,64]{3,2,1,0:T(8,128)(2,1)} %copy.154) | data formatting | bytes 4194304 | tf_op jit(solution)/shard_map/while/body/eval_jaxpr/reshape | solution.py:203
  276.9 2.2 convolution_bitcast_fusion.4
  279.1 1.9 copy.155
  281.0 1.4 constant_dynamic-update-slice_fusion.2
  282.7 0.8 fusion.55
  283.5 8.1 %convert_element_type.203 = bf16[64,32,64,8]{1,0,3,2:T(8,128)(2,1)} reshape(bf16[2048,512]{0,1:T(8,128)(2,1)S(1)} %fusion.55) | data formatting | bytes 4194304 | tf_op jit(solution)/shard_map/while/body/eval_jaxpr/convert_element_type | solution.py:202
  291.6 14.6 %copy.154 = bf16[32,8,64,64]{3,2,1,0:T(8,128)(2,1)} copy(bf16[32,8,64,64]{0,2,1,3:T(8,128)(2,1)} %bitcast.151) | data formatting | bytes 4194304 | tf_op jit(solution)/shard_map/while/body/eval_jaxpr/convert_element_type | solution.py:202
  306.2 5.7 %reshape.383 = bf16[256,4096]{1,0:T(8,128)(2,1)S(1)} reshape(bf16[32,8,64,64]{3,2,1,0:T(8,128)(2,1)} %copy.154) | data formatting | bytes 4194304 | tf_op jit(solution)/shard_map/while/body/eval_jaxpr/reshape | solution.py:203
  311.9 2.2 convolution_bitcast_fusion.4
  314.0 1.9 copy.155
  315.9 1.5 constant_dynamic-update-slice_fusion.2
  317.6 0.8 fusion.55
  318.4 8.1 %convert_element_type.203 = bf16[64,32,64,8]{1,0,3,2:T(8,128)(2,1)} reshape(bf16[2048,512]{0,1:T(8,128)(2,1)S(1)} %fusion.55) | data formatting | bytes 4194304 | tf_op jit(solution)/shard_map/while/body/eval_jaxpr/convert_element_type | solution.py:202
  326.5 14.6 %copy.154 = bf16[32,8,64,64]{3,2,1,0:T(8,128)(2,1)} copy(bf16[32,8,64,64]{0,2,1,3:T(8,128)(2,1)} %bitcast.151) | data formatting | bytes 4194304 | tf_op jit(solution)/shard_map/while/body/eval_jaxpr/convert_element_type | solution.py:202
  341.1 5.7 %reshape.383 = bf16[256,4096]{1,0:T(8,128)(2,1)S(1)} reshape(bf16[32,8,64,64]{3,2,1,0:T(8,128)(2,1)} %copy.154) | data formatting | bytes 4194304 | tf_op jit(solution)/shard_map/while/body/eval_jaxpr/reshape | solution.py:203
  346.8 2.2 convolution_bitcast_fusion.4
  349.0 1.9 copy.155
  350.9 1.5 constant_dynamic-update-slice_fusion.2
  352.4 0.7 copy.126
  353.2 69.3 %reduce-scatter.2.cloned.1.call-done = f32[4,32,4096]{2,1,0:T(8,128)} async-done(((f32[4,128,4096]{2,1,0:T(8,128)}), f32[4,32,4096]{2,1,0:T(8,128)}) %reduce-scatter.2.cloned.1.call-update) | async-done | bytes 2097168 | tf_op jit(solution)/shard_map/reduce_scatter | solution.py:208
  422.5 3.0 fusion.5
  (111 shorter events, 10.0 us)
Async XLA Ops:
  7.2 119.1 %copy-start = (bf16[4,256,64]{1,2,0:T(8,128)(2,1)S(1)}, bf16[4,256,64]{1,2,0:T(8,128)(2,1)}, u32[]{:S(2)}) copy-start(bf16[4,256,64]{1,2,0:T(8,128)(2,1)} %param.24) | copy-start | bytes 393220
  7.2 61.7 %copy-start.17 = (u32[32]{0:T(128)S(1)}, u32[32]{0:T(128)}, u32[]{:S(2)}) copy-start(u32[32]{0:T(128)} %constant.112) | copy-start | bytes 388
  7.2 63.9 %copy-start.1 = (bf16[4,32,4096]{2,1,0:T(8,128)(2,1)S(1)}, bf16[4,32,4096]{2,1,0:T(8,128)(2,1)}, u32[]{:S(2)}) copy-start(bf16[4,32,4096]{2,1,0:T(8,128)(2,1)} %param.19) | copy-start | bytes 3145732
  7.2 44.7 %copy-start.13 = (s32[1,4]{1,0:T(1,128)S(1)}, s32[1,4]{1,0:T(1,128)}, u32[]{:S(2)}) copy-start(s32[1,4]{1,0:T(1,128)} %param.21) | copy-start | bytes 52
  7.2 61.6 %copy-start.15 = (f32[8]{0:T(128)S(1)}, f32[8]{0:T(128)}, u32[]{:S(2)}) copy-start(f32[8]{0:T(128)} %param.26) | copy-start | bytes 100
  7.2 63.9 %copy-start.16 = (f32[32]{0:T(128)S(1)}, f32[32]{0:T(128)}, u32[]{:S(2)}) copy-start(f32[32]{0:T(128)} %param.27) | copy-start | bytes 388
  7.2 63.9 %copy-start.14 = (f32[32,8]{0,1:T(8,128)S(1)}, f32[32,8]{0,1:T(8,128)}, u32[]{:S(2)}) copy-start(f32[32,8]{0,1:T(8,128)} %param.28) | copy-start | bytes 3076
  7.2 118.3 %all-to-all-start = ((bf16[8,64,256]{2,1,0:T(8,128)(2,1)}), bf16[8,64,256]{2,1,0:T(8,128)(2,1)S(1)}, u32[]{:S(2)}, u32[]{:S(2)}) async-start(bf16[8,64,256]{2,1,0:T(8,128)(2,1)} %param.18), calls=%async_computation | async-start | bytes 524288 | tf_op jit(solution)/shard_map/all_to_all | solution.py:69
  14.7 55.5 %all-reduce.6.cloned.1.call-start = ((), (), s32[]{:S(2)}) async-start(), calls=%async_computation.4 | async-start | bytes 262144 | tf_op jit(solution)/shard_map/psum | solution.py:50
  123.6 2.5 copy-start.9
  133.5 1.0 copy-start.3
  133.5 1.1 copy-start.4
  134.6 0.8 copy-start.6
  135.7 2.0 collective-permute-start
  137.7 21.9 %copy-start.5 = (bf16[128,32,8]{0,2,1:T(8,128)(2,1)S(1)}, bf16[128,32,8]{0,2,1:T(8,128)(2,1)}, u32[]{:S(2)}) copy-start(bf16[128,32,8]{0,2,1:T(8,128)(2,1)} %param.32) | copy-start | bytes 196612
  137.7 22.0 %copy-start.12 = (s32[1,4]{1,0:T(1,128)S(1)}, s32[1,4]{1,0:T(1,128)}, u32[]{:S(2)}) copy-start(s32[1,4]{1,0:T(1,128)} %param.20) | copy-start | bytes 52
  137.7 14.0 %collective-permute-start.1 = (f32[512,256]{1,0:T(8,128)S(1)}, f32[512,256]{1,0:T(8,128)S(1)}, u32[]{:S(2)}, u32[]{:S(2)}) collective-permute-start(f32[512,256]{1,0:T(8,128)S(1)} %add.120), channel_id=1, source_target_pairs={{0,2},{1,3},{2,0},{3,1},{4,6},{5,7},{6,4},{7,5},{8,10},{9,11},{10,... | collective-permute-start | bytes 1572872 | tf_op jit(solution)/shard_map/ppermute | solution.py:144
  155.0 22.4 %copy-start.10 = (f32[256]{0:T(256)S(1)}, f32[256]{0:T(256)}, u32[]{:S(2)}) copy-start(f32[256]{0:T(256)} %param.29) | copy-start | bytes 3076
  155.8 21.9 %copy-start.8 = (bf16[256,8]{0,1:T(8,128)(2,1)S(1)}, bf16[256,8]{0,1:T(8,128)(2,1)}, u32[]{:S(2)}) copy-start(bf16[256,8]{0,1:T(8,128)(2,1)} %param.31) | copy-start | bytes 12292
  155.8 12.1 %all-to-all-start.1 = ((bf16[8,2,8192]{2,1,0:T(2,128)(2,1)}), bf16[8,2,8192]{2,1,0:T(2,128)(2,1)S(1)}, u32[]{:S(2)}, u32[]{:S(2)}) async-start(bf16[8,2,8192]{2,1,0:T(2,128)(2,1)} %reshape.378), calls=%async_computation.1 | async-start | bytes 524288 | tf_op jit(solution)/shard_map/all_to_all | solution.py:152
  159.4 263.2 %reduce-scatter.2.cloned.1.call-start = ((), (), s32[]{:S(2)}) async-start(), calls=%async_computation.3 | async-start | bytes 10485760 | tf_op jit(solution)/shard_map/reduce_scatter | solution.py:208
  168.2 43.1 %copy-start.7 = (bf16[256,32]{0,1:T(8,128)(2,1)S(1)}, bf16[256,32]{0,1:T(8,128)(2,1)}, u32[]{:S(2)}) copy-start(bf16[256,32]{0,1:T(8,128)(2,1)} %param.30) | copy-start | bytes 49156
  352.4 70.1 %copy-start.2 = (bf16[4,32,4096]{2,1,0:T(8,128)(2,1)S(1)}, bf16[4,32,4096]{2,1,0:T(8,128)(2,1)}, u32[]{:S(2)}) copy-start(bf16[4,32,4096]{2,1,0:T(8,128)(2,1)} %param.19) | copy-start | bytes 3145732
  352.4 70.1 %copy-start.11 = (f32[32]{0:T(128)S(1)}, f32[32]{0:T(128)}, u32[]{:S(2)}) copy-start(f32[32]{0:T(128)} %param.33) | copy-start | bytes 388
Sparse Core Ops, SparseCore 0:
  18.5 33.1 all-reduce.5
  352.5 69.9 reduce-scatter.1
